TPU v7x, 32 devices: a whole 2x2x4 slice. The times are simulated.
32 devices in a mesh: groups: 2 (over y), blk: 4 (over z), head: 2 (over x), rep: 2 (over core).
Axes of the slice: x: 2, y: 2, z: 4, core: 2. Of those that a mesh axis runs over, the one named last changes fastest.
Arguments:
- query: bfloat16 [128, 16384], P(('groups', 'blk', 'rep'), 'head'), parts along dimension 0, may hold values from -200 to 200
- keys: bfloat16 [8, 2, 2048, 8, 128], P(('groups', 'blk'), 'rep', None, 'head'), parts along dimension 0, may hold values from -8 to 8
- values: bfloat16 [8, 2, 2048, 8, 128], P(('groups', 'blk'), 'rep', None, 'head'), parts along dimension 0, may hold values from -6 to 6
- lengths: int32 [128], P('groups'), parts along dimension 0, may hold values from 2 to 8192, as said below
- out_weight: bfloat16 [16384, 16384], P('head', ('blk', 'rep')), may hold values from -0.046875 to 0.046875
Outputs:
- projected: bfloat16 [128, 16384], P(('groups', 'head'), ('blk', 'rep')), parts along dimension 0
There are 2 independent parts, one for each index of `groups`. A program takes and returns all parts, laid end to end along the dimension named above; an argument that names none is the same for every part. Nothing has to cross between parts.
Inputs may be any that keep to these rules, and one draw needn't show every extreme that they name: `lengths`: some request of every draw sees all 8192 positions.
All inputs are finite; a program needn't handle non-finite values.
Results may differ from a plain program's by a relative error of at most 0.012.
Values may be sent and summed in bfloat16 or wider, within the bound.
A program may use at most 128 MiB of HBM per device.

v0:
```python
import jax
import jax.numpy as jnp
from jax import lax
from jax.sharding import PartitionSpec as P

NEG = -1e30


def shifted(x, axis, by):
    devices = lax.axis_size(axis)
    return lax.ppermute(x, axis, [(i, (i + by) % devices) for i in range(devices)])


def stop_partial(visiting, row_lengths, positions, key_slot, value_slot, score_scale):
    row_count = visiting.shape[0]
    kv_heads = key_slot.shape[1]
    head_dim = key_slot.shape[2]
    queries = visiting.reshape(row_count, kv_heads, -1, head_dim)
    scores = (
        jnp.einsum("rkgd,jkd->rkgj", queries, key_slot, preferred_element_type=jnp.float32)
        * score_scale
    )
    live_mask = (positions[None, :] < row_lengths[:, None])[:, None, None, :]
    best_score = jnp.max(jnp.where(live_mask, scores, NEG), axis=-1)
    weights = jnp.where(live_mask, jnp.exp(scores - best_score[..., None]), 0.0)
    block_sum = jnp.sum(weights, axis=-1)
    partial_value = jnp.einsum(
        "rkgj,jkd->rkgd",
        weights.astype(jnp.bfloat16),
        value_slot,
        preferred_element_type=jnp.float32,
    )
    return (partial_value.astype(jnp.bfloat16), best_score, block_sum)


def body(query, keys, values, lengths, out_weight):
    row_count = query.shape[0]
    slab_len = keys.shape[2]
    head_dim = keys.shape[4]
    score_scale = head_dim ** (-0.5)
    blocks = lax.axis_size("blk")
    replicas = lax.axis_size("rep")
    span_count = min(8, blocks)
    stride = blocks // span_count
    holder = lax.axis_index("blk")
    rep_index = lax.axis_index("rep")
    key_slot = keys[0, 0]
    value_slot = values[0, 0]
    positions = holder // stride * slab_len + jnp.arange(slab_len, dtype=jnp.int32)
    visiting = query
    stored = []
    for stop_index in range(span_count):
        if stop_index > 0:
            visiting = shifted(visiting, "blk", stride)
        owner_index = (holder - stop_index * stride) % blocks
        first_row = (owner_index * replicas + rep_index) * row_count
        row_lengths = lax.dynamic_slice_in_dim(lengths, first_row, row_count, 0)
        stop_piece = stop_partial(
            visiting, row_lengths, positions, key_slot, value_slot, score_scale
        )
        stored.append(stop_piece)
    outs_home = [stored[0][0]]
    best_home = [stored[0][1]]
    sums_home = [stored[0][2]]
    for stop_index in range(1, span_count):
        outs_home.append(shifted(stored[stop_index][0], "blk", -stop_index * stride))
        stats_home = shifted(
            (stored[stop_index][1], stored[stop_index][2]), "blk", -stop_index * stride
        )
        best_home.append(stats_home[0])
        sums_home.append(stats_home[1])
    best_all = jnp.stack(best_home)
    overall = jnp.max(best_all, axis=0)
    factors = jnp.exp(best_all - overall[None])
    total_sum = jnp.sum(factors * jnp.stack(sums_home), axis=0)
    total_out = jnp.sum(factors[..., None] * jnp.stack(outs_home).astype(jnp.float32), axis=0)
    attended = (total_out / total_sum[..., None]).astype(jnp.bfloat16).reshape(row_count, -1)
    gathered = lax.all_gather(attended, ("blk", "rep"), axis=0, tiled=True)
    projected = lax.psum_scatter(
        jnp.dot(gathered, out_weight, preferred_element_type=jnp.float32),
        "head",
        scatter_dimension=0,
        tiled=True,
    )
    return projected.astype(jnp.bfloat16)


def solution(mesh):
    return jax.shard_map(
        body,
        mesh=mesh,
        in_specs=(
            P(("groups", "blk", "rep"), "head"),
            P(("groups", "blk"), "rep", None, "head", None),
            P(("groups", "blk"), "rep", None, "head", None),
            P("groups"),
            P("head", ("blk", "rep")),
        ),
        out_specs=P(("groups", "head"), ("blk", "rep")),
        check_vma=False,
    )
```

profile of v0, /device:TPU:0, one launch (start us, length us, event | category | flops | bytes accessed | tf_op | source)
XLA Modules:
  0.0 113.8 jit_solution(224056178729096985)
XLA Ops:
  6.5 3.1 %collective-permute-start = (bf16[8,8192]{1,0:T(8,128)(2,1)}, bf16[8,8192]{1,0:T(8,128)(2,1)S(1)}, u32[]{:S(2)}, u32[]{:S(2)}) collective-permute-start(bf16[8,8192]{1,0:T(8,128)(2,1)} %param.5), channel_id=1, source_target_pairs={{0,4},{4,8},{8,12},{12,0},{1,5},{5,9},{9,13},{13,1},{2,6},{6,10},{... | collective-permute-start | bytes 393224 | tf_op jit(solution)/shard_map/ppermute | solution.py:11
  10.6 2.7 %fusion.9 = (f32[8,4,16]{2,0,1:T(8,128)S(1)}, f32[4,2048,8,16]{1,3,2,0:T(8,128)S(1)}) fusion(pred[8,2048]{1,0:T(8,128)(4,1)S(1)} %get-tuple-element.7, bf16[8,4,16,128]{3,0,2,1:T(8,128)(2,1)} %bitcast.149, bf16[2048,4,128,1]{2,1,0,3:T(4,128)(2,1)} %bitcast.145), kind=kOutput, calls=%fused_computation.17 | convolution fusion | flops 271580672 | bytes 6440960 | tf_op jit(solution)/shard_map/rkgd,jkd->rkgj/dot_general | solution.py:20
  13.3 1.2 %fusion.91 = bf16[1,8,4,16,128]{4,3,1,2,0:T(8,128)(2,1)S(1)} fusion(bf16[2048,4,128,1]{2,1,0,3:T(4,128)(2,1)S(1)} %bitcast.122, f32[4,2048,8,16]{1,3,2,0:T(8,128)S(1)} %get-tuple-element.22, f32[8,4,16]{2,0,1:T(8,128)S(1)} %get-tuple-element.21, pred[8,2048]{1,0:T(8,128)(4,1)S(1)} %get-tuple-element.7), kind=kOutput, calls=%fused_computation.67 | convolution fusion | flops 272695296 | bytes 6440960 | tf_op jit(solution)/shard_map/rkgj,jkd->rkgd/dot_general | solution.py:27
  14.6 1.1 fusion.12
  17.3 1.2 %fusion.86 = bf16[8,4,16,128]{3,2,0,1:T(8,128)(2,1)S(1)} fusion(bf16[2048,4,128,1]{2,1,0,3:T(4,128)(2,1)S(1)} %bitcast.125, f32[4,2048,8,16]{1,3,2,0:T(8,128)S(1)} %get-tuple-element.20, f32[8,4,16]{2,0,1:T(8,128)S(1)} %get-tuple-element.19, pred[8,2048]{1,0:T(8,128)(4,1)S(1)} %get-tuple-element.8), kind=kOutput, calls=%fused_computation.66 | convolution fusion | flops 272695296 | bytes 6440960 | tf_op jit(solution)/shard_map/rkgj,jkd->rkgd/dot_general | solution.py:27
  18.5 1.6 %collective-permute-start.2 = (bf16[8,8192]{1,0:T(8,128)(2,1)S(1)}, bf16[8,8192]{1,0:T(8,128)(2,1)S(1)}, u32[]{:S(2)}, u32[]{:S(2)}) collective-permute-start(bf16[8,8192]{1,0:T(8,128)(2,1)S(1)} %collective-permute-done), channel_id=1, source_target_pairs={{0,4},{4,8},{8,12},{12,0},{1,5},{5,9},{9,13},{13,1},{2,6},{6,10},{... | collective-permute-start | bytes 393224 | tf_op jit(solution)/shard_map/ppermute | solution.py:11
  21.2 2.3 %collective-permute-start.1 = (f32[8,4,16]{2,0,1:T(8,128)S(1)}, f32[8,4,16]{2,0,1:T(8,128)S(1)}, u32[]{:S(2)}, u32[]{:S(2)}) collective-permute-start(f32[8,4,16]{2,0,1:T(8,128)S(1)} %get-tuple-element.19), channel_id=1, source_target_pairs={{0,12},{4,0},{8,4},{12,8},{1,13},{5,1},{9,5},{13,9},{2,14},{6,2},{... | collective-permute-start | bytes 6152 | tf_op jit(solution)/shard_map/ppermute | solution.py:11
  23.8 2.0 %collective-permute-start.6 = (bf16[8,4,16,128]{3,2,0,1:T(8,128)(2,1)S(1)}, bf16[8,4,16,128]{3,2,0,1:T(8,128)(2,1)S(1)}, u32[]{:S(2)}, u32[]{:S(2)}) collective-permute-start(bf16[8,4,16,128]{3,2,0,1:T(8,128)(2,1)S(1)} %fusion.86), channel_id=1, source_target_pairs={{0,12},{4,0},{8,4},{12,8},{1,13},{5,1},{9,5},{13,9},{2,14},{6,2},{... | collective-permute-start | bytes 393224 | tf_op jit(solution)/shard_map/ppermute | solution.py:11
  25.8 1.1 fusion.3
  26.9 1.2 %fusion.81 = bf16[8,4,16,128]{3,2,0,1:T(8,128)(2,1)S(1)} fusion(bf16[2048,4,128,1]{2,1,0,3:T(4,128)(2,1)S(1)} %bitcast.124, f32[4,2048,8,16]{1,3,2,0:T(8,128)S(1)} %get-tuple-element.18, f32[8,4,16]{2,0,1:T(8,128)S(1)} %get-tuple-element.17, pred[8,2048]{1,0:T(8,128)(4,1)S(1)} %get-tuple-element.9), kind=kOutput, calls=%fused_computation.65 | convolution fusion | flops 272695296 | bytes 6440960 | tf_op jit(solution)/shard_map/rkgj,jkd->rkgd/dot_general | solution.py:27
  29.5 1.2 %collective-permute-start.3 = (f32[8,4,16]{2,0,1:T(8,128)S(1)}, f32[8,4,16]{2,0,1:T(8,128)S(1)}, u32[]{:S(2)}, u32[]{:S(2)}) collective-permute-start(f32[8,4,16]{2,0,1:T(8,128)S(1)} %get-tuple-element.17), channel_id=1, source_target_pairs={{0,8},{4,12},{8,0},{12,4},{1,9},{5,13},{9,1},{13,5},{2,10},{6,14},... | collective-permute-start | bytes 6152 | tf_op jit(solution)/shard_map/ppermute | solution.py:11
  30.8 4.5 %collective-permute-done.4 = bf16[8,8192]{1,0:T(8,128)(2,1)S(1)} collective-permute-done((bf16[8,8192]{1,0:T(8,128)(2,1)S(1)}, bf16[8,8192]{1,0:T(8,128)(2,1)S(1)}, u32[]{:S(2)}, u32[]{:S(2)}) %collective-permute-start.4) | collective-permute-done | bytes 131104 | tf_op jit(solution)/shard_map/ppermute | solution.py:11
  35.3 1.1 fusion
  36.5 1.2 %fusion.76 = bf16[8,4,16,128]{3,2,0,1:T(8,128)(2,1)S(1)} fusion(bf16[2048,4,128,1]{2,1,0,3:T(4,128)(2,1)S(1)} %bitcast.123, f32[4,2048,8,16]{1,3,2,0:T(8,128)S(1)} %get-tuple-element.16, f32[8,4,16]{2,0,1:T(8,128)S(1)} %get-tuple-element.15, pred[8,2048]{1,0:T(8,128)(4,1)S(1)} %get-tuple-element.10), kind=kOutput, calls=%fused_computation.64 | convolution fusion | flops 272695296 | bytes 6440960 | tf_op jit(solution)/shard_map/rkgj,jkd->rkgd/dot_general | solution.py:27
  37.7 1.1 fusion.18
  39.0 2.8 %collective-permute-start.7 = (bf16[8,4,16,128]{3,2,0,1:T(8,128)(2,1)S(1)}, bf16[8,4,16,128]{3,2,0,1:T(8,128)(2,1)S(1)}, u32[]{:S(2)}, u32[]{:S(2)}) collective-permute-start(bf16[8,4,16,128]{3,2,0,1:T(8,128)(2,1)S(1)} %fusion.81), channel_id=1, source_target_pairs={{0,8},{4,12},{8,0},{12,4},{1,9},{5,13},{9,1},{13,5},{2,10},{6,14},... | collective-permute-start | bytes 393224 | tf_op jit(solution)/shard_map/ppermute | solution.py:11
  42.1 1.2 %collective-permute-start.11 = (f32[8,4,16]{2,0,1:T(8,128)S(1)}, f32[8,4,16]{2,0,1:T(8,128)S(1)}, u32[]{:S(2)}, u32[]{:S(2)}) collective-permute-start(f32[8,4,16]{2,0,1:T(8,128)S(1)} %fusion.18), channel_id=1, source_target_pairs={{0,4},{4,8},{8,12},{12,0},{1,5},{5,9},{9,13},{13,1},{2,6},{6,10},{... | collective-permute-start | bytes 6152 | tf_op jit(solution)/shard_map/ppermute | solution.py:11
  43.4 2.8 %collective-permute-done.10 = f32[8,4,16]{2,0,1:T(8,128)S(1)} collective-permute-done((f32[8,4,16]{2,0,1:T(8,128)S(1)}, f32[8,4,16]{2,0,1:T(8,128)S(1)}, u32[]{:S(2)}, u32[]{:S(2)}) %collective-permute-start.10) | collective-permute-done | bytes 2080 | tf_op jit(solution)/shard_map/ppermute | solution.py:11
  46.2 2.6 %collective-permute-done.11 = f32[8,4,16]{2,0,1:T(8,128)S(1)} collective-permute-done((f32[8,4,16]{2,0,1:T(8,128)S(1)}, f32[8,4,16]{2,0,1:T(8,128)S(1)}, u32[]{:S(2)}, u32[]{:S(2)}) %collective-permute-start.11) | collective-permute-done | bytes 2080 | tf_op jit(solution)/shard_map/ppermute | solution.py:11
  48.9 1.7 %collective-permute-done.7 = bf16[8,4,16,128]{3,2,0,1:T(8,128)(2,1)S(1)} collective-permute-done((bf16[8,4,16,128]{3,2,0,1:T(8,128)(2,1)S(1)}, bf16[8,4,16,128]{3,2,0,1:T(8,128)(2,1)S(1)}, u32[]{:S(2)}, u32[]{:S(2)}) %collective-permute-start.7) | collective-permute-done | bytes 131104 | tf_op jit(solution)/shard_map/ppermute | solution.py:11
  51.9 21.4 %all-gather.2.cloned.1.call-done = bf16[64,8192]{1,0:T(8,128)(2,1)} async-done(((bf16[8,8192]{1,0:T(8,128)(2,1)}), bf16[64,8192]{1,0:T(8,128)(2,1)}) %all-gather.2.cloned.1.call-update) | async-done | bytes 1048592 | tf_op jit(solution)/shard_map/all_gather | solution.py:78
  73.3 17.6 %fusion.112 = f32[64,2048]{1,0:T(8,128)} fusion(bf16[64,8192]{1,0:T(8,128)(2,1)} %all-gather.2.cloned.1.call-done, bf16[8192,2048]{1,0:T(8,128)(2,1)} %param.9), kind=kOutput, calls=%fused_computation.94 | convolution fusion | flops 2147483648 | bytes 35127296 | tf_op jit(solution)/shard_map/dot_general | solution.py:80
  91.0 14.4 %reduce-scatter.2.cloned.1.call-done = f32[32,2048]{1,0:T(8,128)} async-done(((f32[64,2048]{1,0:T(8,128)}), f32[32,2048]{1,0:T(8,128)}) %reduce-scatter.2.cloned.1.call-update) | async-done | bytes 262160 | tf_op jit(solution)/shard_map/reduce_scatter | solution.py:79
  105.4 1.6 %convert_element_type.64 = bf16[32,2048]{1,0:T(8,128)(2,1)} convert(f32[32,2048]{1,0:T(8,128)} %reduce-scatter.2.cloned.1.call-done) | non-fusion elementwise | flops 65536 | bytes 393216 | tf_op jit(solution)/shard_map/convert_element_type | solution.py:85
  (36 shorter events, 7.3 us)
Async XLA Ops:
  6.5 6.8 %copy-start = (bf16[1,1,2048,4,128]{4,3,2,1,0:T(4,128)(2,1)S(1)}, bf16[1,1,2048,4,128]{4,3,2,1,0:T(4,128)(2,1)}, u32[]{:S(2)}) copy-start(bf16[1,1,2048,4,128]{4,3,2,1,0:T(4,128)(2,1)} %param.7) | copy-start | bytes 6291460
  6.5 66.8 %all-gather.2.cloned.1.call-start = ((), (), s32[]{:S(2)}) async-start(), calls=%async_computation.1 | async-start | bytes 1179648 | tf_op jit(solution)/shard_map/all_gather | solution.py:78
  6.5 9.1 %collective-permute-start = (bf16[8,8192]{1,0:T(8,128)(2,1)}, bf16[8,8192]{1,0:T(8,128)(2,1)S(1)}, u32[]{:S(2)}, u32[]{:S(2)}) collective-permute-start(bf16[8,8192]{1,0:T(8,128)(2,1)} %param.5), channel_id=1, source_target_pairs={{0,4},{4,8},{8,12},{12,0},{1,5},{5,9},{9,13},{13,1},{2,6},{6,10},{... | collective-permute-start | bytes 393224 | tf_op jit(solution)/shard_map/ppermute | solution.py:11
  14.5 1.6 %copy-start.1 = (bf16[1,1,2048,4,128]{4,3,2,1,0:T(4,128)(2,1)S(1)}, bf16[1,1,2048,4,128]{4,3,2,1,0:T(4,128)(2,1)}, u32[]{:S(2)}) copy-start(bf16[1,1,2048,4,128]{4,3,2,1,0:T(4,128)(2,1)} %param.6) | copy-start | bytes 6291460
  18.5 7.3 %collective-permute-start.2 = (bf16[8,8192]{1,0:T(8,128)(2,1)S(1)}, bf16[8,8192]{1,0:T(8,128)(2,1)S(1)}, u32[]{:S(2)}, u32[]{:S(2)}) collective-permute-start(bf16[8,8192]{1,0:T(8,128)(2,1)S(1)} %collective-permute-done), channel_id=1, source_target_pairs={{0,4},{4,8},{8,12},{12,0},{1,5},{5,9},{9,13},{13,1},{2,6},{6,10},{... | collective-permute-start | bytes 393224 | tf_op jit(solution)/shard_map/ppermute | solution.py:11
  21.2 17.6 %collective-permute-start.1 = (f32[8,4,16]{2,0,1:T(8,128)S(1)}, f32[8,4,16]{2,0,1:T(8,128)S(1)}, u32[]{:S(2)}, u32[]{:S(2)}) collective-permute-start(f32[8,4,16]{2,0,1:T(8,128)S(1)} %get-tuple-element.19), channel_id=1, source_target_pairs={{0,12},{4,0},{8,4},{12,8},{1,13},{5,1},{9,5},{13,9},{2,14},{6,2},{... | collective-permute-start | bytes 6152 | tf_op jit(solution)/shard_map/ppermute | solution.py:11
  23.5 19.8 %collective-permute-start.9 = (f32[8,4,16]{2,0,1:T(8,128)S(1)}, f32[8,4,16]{2,0,1:T(8,128)S(1)}, u32[]{:S(2)}, u32[]{:S(2)}) collective-permute-start(f32[8,4,16]{2,0,1:T(8,128)S(1)} %fusion.14), channel_id=1, source_target_pairs={{0,12},{4,0},{8,4},{12,8},{1,13},{5,1},{9,5},{13,9},{2,14},{6,2},{... | collective-permute-start | bytes 6152 | tf_op jit(solution)/shard_map/ppermute | solution.py:11
  23.8 25.0 %collective-permute-start.6 = (bf16[8,4,16,128]{3,2,0,1:T(8,128)(2,1)S(1)}, bf16[8,4,16,128]{3,2,0,1:T(8,128)(2,1)S(1)}, u32[]{:S(2)}, u32[]{:S(2)}) collective-permute-start(bf16[8,4,16,128]{3,2,0,1:T(8,128)(2,1)S(1)} %fusion.86), channel_id=1, source_target_pairs={{0,12},{4,0},{8,4},{12,8},{1,13},{5,1},{9,5},{13,9},{2,14},{6,2},{... | collective-permute-start | bytes 393224 | tf_op jit(solution)/shard_map/ppermute | solution.py:11
  28.2 7.1 %collective-permute-start.4 = (bf16[8,8192]{1,0:T(8,128)(2,1)S(1)}, bf16[8,8192]{1,0:T(8,128)(2,1)S(1)}, u32[]{:S(2)}, u32[]{:S(2)}) collective-permute-start(bf16[8,8192]{1,0:T(8,128)(2,1)S(1)} %collective-permute-done.2), channel_id=1, source_target_pairs={{0,4},{4,8},{8,12},{12,0},{1,5},{5,9},{9,13},{13,1},{2,6},{6,10},{... | collective-permute-start | bytes 393224 | tf_op jit(solution)/shard_map/ppermute | solution.py:11
  29.5 9.4 %collective-permute-start.3 = (f32[8,4,16]{2,0,1:T(8,128)S(1)}, f32[8,4,16]{2,0,1:T(8,128)S(1)}, u32[]{:S(2)}, u32[]{:S(2)}) collective-permute-start(f32[8,4,16]{2,0,1:T(8,128)S(1)} %get-tuple-element.17), channel_id=1, source_target_pairs={{0,8},{4,12},{8,0},{12,4},{1,9},{5,13},{9,1},{13,5},{2,10},{6,14},... | collective-permute-start | bytes 6152 | tf_op jit(solution)/shard_map/ppermute | solution.py:11
  36.4 5.7 %collective-permute-start.5 = (f32[8,4,16]{2,0,1:T(8,128)S(1)}, f32[8,4,16]{2,0,1:T(8,128)S(1)}, u32[]{:S(2)}, u32[]{:S(2)}) collective-permute-start(f32[8,4,16]{2,0,1:T(8,128)S(1)} %get-tuple-element.15), channel_id=1, source_target_pairs={{0,4},{4,8},{8,12},{12,0},{1,5},{5,9},{9,13},{13,1},{2,6},{6,10},{... | collective-permute-start | bytes 6152 | tf_op jit(solution)/shard_map/ppermute | solution.py:11
  38.8 7.4 %collective-permute-start.10 = (f32[8,4,16]{2,0,1:T(8,128)S(1)}, f32[8,4,16]{2,0,1:T(8,128)S(1)}, u32[]{:S(2)}, u32[]{:S(2)}) collective-permute-start(f32[8,4,16]{2,0,1:T(8,128)S(1)} %fusion.16), channel_id=1, source_target_pairs={{0,8},{4,12},{8,0},{12,4},{1,9},{5,13},{9,1},{13,5},{2,10},{6,14},... | collective-permute-start | bytes 6152 | tf_op jit(solution)/shard_map/ppermute | solution.py:11
  39.0 11.6 %collective-permute-start.7 = (bf16[8,4,16,128]{3,2,0,1:T(8,128)(2,1)S(1)}, bf16[8,4,16,128]{3,2,0,1:T(8,128)(2,1)S(1)}, u32[]{:S(2)}, u32[]{:S(2)}) collective-permute-start(bf16[8,4,16,128]{3,2,0,1:T(8,128)(2,1)S(1)} %fusion.81), channel_id=1, source_target_pairs={{0,8},{4,12},{8,0},{12,4},{1,9},{5,13},{9,1},{13,5},{2,10},{6,14},... | collective-permute-start | bytes 393224 | tf_op jit(solution)/shard_map/ppermute | solution.py:11
  42.1 6.7 %collective-permute-start.11 = (f32[8,4,16]{2,0,1:T(8,128)S(1)}, f32[8,4,16]{2,0,1:T(8,128)S(1)}, u32[]{:S(2)}, u32[]{:S(2)}) collective-permute-start(f32[8,4,16]{2,0,1:T(8,128)S(1)} %fusion.18), channel_id=1, source_target_pairs={{0,4},{4,8},{8,12},{12,0},{1,5},{5,9},{9,13},{13,1},{2,6},{6,10},{... | collective-permute-start | bytes 6152 | tf_op jit(solution)/shard_map/ppermute | solution.py:11
  43.3 7.3 %collective-permute-start.8 = (bf16[8,4,16,128]{3,2,0,1:T(8,128)(2,1)S(1)}, bf16[8,4,16,128]{3,2,0,1:T(8,128)(2,1)S(1)}, u32[]{:S(2)}, u32[]{:S(2)}) collective-permute-start(bf16[8,4,16,128]{3,2,0,1:T(8,128)(2,1)S(1)} %fusion.76), channel_id=1, source_target_pairs={{0,4},{4,8},{8,12},{12,0},{1,5},{5,9},{9,13},{13,1},{2,6},{6,10},{... | collective-permute-start | bytes 393224 | tf_op jit(solution)/shard_map/ppermute | solution.py:11
  51.9 53.5 %reduce-scatter.2.cloned.1.call-start = ((), (), s32[]{:S(2)}) async-start(), calls=%async_computation.2 | async-start | bytes 786432 | tf_op jit(solution)/shard_map/reduce_scatter | solution.py:79
Sparse Core Ops, SparseCore 0:
  52.0 21.2 all-gather.1
  91.1 14.2 reduce-scatter.1
where the time goes:
time: 114 us
  waiting for transfers between devices  47.8 us (42%)
  matrix products  28.6 us (25%)
  starting transfers between devices  15 us (13%)
  between operations  13.5 us (12%)
  other arithmetic  6.66 us (6%)
  local copies, waits for them, and re-layouts  2.15 us (2%)
    all_gather x1, waiting for transfers between devices, body(): gathered = lax.all_gather(attended, ('blk', 'rep'), axis=0, tiled=True)  21.4 us
    dot_general x1, matrix products, body(): jnp.dot(gathered, out_weight, preferred_element_type=jnp.float32)  17.6 us
    ppermute x12, starting transfers between devices, shifted(): lax.ppermute(x, axis, [(i, (i + by) % devices) for i in range(devices)])  15 us
    reduce_scatter x1, waiting for transfers between devices, body(): lax.psum_scatter(jnp.dot(gathered, out_weight, preferred_element_type=jnp...  14.4 us
    ppermute x12, waiting for transfers between devices, shifted(): lax.ppermute(x, axis, [(i, (i + by) % devices) for i in range(devices)])  12 us
    dot_general x4, matrix products, stop_partial(): jnp.einsum('rkgd,jkd->rkgj', queries, key_slot, preferred_element_type=jn...  6.03 us
    dot_general x4, matrix products, stop_partial(): jnp.einsum('rkgj,jkd->rkgd', weights.astype(jnp.bfloat16), value_slot, pr...  4.97 us
    reduce_sum x4, other arithmetic, stop_partial(): block_sum = jnp.sum(weights, axis=-1)  4.42 us
  transfers between devices with their start and end apart: 14, of which 7 were waited for; matrix products, arithmetic and copies ran while one was open for 12% of the time, Pallas kernels for 0%

commit v1 on v0

--- a/solution.py
+++ b/solution.py
@@ -75,7 +75,16 @@
     total_sum = jnp.sum(factors * jnp.stack(sums_home), axis=0)
     total_out = jnp.sum(factors[..., None] * jnp.stack(outs_home).astype(jnp.float32), axis=0)
     attended = (total_out / total_sum[..., None]).astype(jnp.bfloat16).reshape(row_count, -1)
-    gathered = lax.all_gather(attended, ("blk", "rep"), axis=0, tiled=True)
+    a_next, z = (lax.axis_size(("blk", "rep")), lax.axis_index(("blk", "rep")))
+    gathered, clean = (attended, 1)
+    while clean < a_next:
+        next_value = lax.ppermute(
+            gathered, ("blk", "rep"), [(j0, j0 ^ clean) for j0 in range(a_next)]
+        )
+        extra = jnp.concatenate([gathered, next_value], 0)
+        built = jnp.concatenate([next_value, gathered], 0)
+        gathered = jnp.where(z & clean == 0, extra, built)
+        clean = 2 * clean
     projected = lax.psum_scatter(
         jnp.dot(gathered, out_weight, preferred_element_type=jnp.float32),
         "head",

time: 114 us -> 123 us (1.079)
  waiting for transfers between devices: 47.8 us -> 59.8 us
  matrix products: 28.6 us -> 25.4 us
    ppermute x0 -> x3, waiting for transfers between devices: none -> 33.9 us  [body(): lax.ppermute(gathered, ('blk', 'rep'), [(j0, j0 ^ clean) for j0 in range(...]
    all_gather x1 -> x0, waiting for transfers between devices: 21.4 us -> none  [body(): gathered = lax.all_gather(attended, ('blk', 'rep'), axis=0, tiled=True)]
    dot_general x1, matrix products: 17.6 us -> 14.4 us  [body(): jnp.dot(gathered, out_weight, preferred_element_type=jnp.float32)]
  transfers between devices with their start and end apart: 14 -> 16, of which waited for: 7 -> 9; matrix products, arithmetic and copies ran while one was open for 12% -> 11% of each run, Pallas kernels for 0% -> 0%
where the time goes in v1:
time: 123 us
  waiting for transfers between devices  59.8 us (49%)
  matrix products  25.4 us (21%)
  starting transfers between devices  16.2 us (13%)
  between operations  13.6 us (11%)
  other arithmetic  6.79 us (6%)
  local copies, waits for them, and re-layouts  1.49 us (1%)
    ppermute x3, waiting for transfers between devices, body(): lax.ppermute(gathered, ('blk', 'rep'), [(j0, j0 ^ clean) for j0 in range(...  33.9 us
    ppermute x12, starting transfers between devices, shifted(): lax.ppermute(x, axis, [(i, (i + by) % devices) for i in range(devices)])  15 us
    dot_general x1, matrix products, body(): jnp.dot(gathered, out_weight, preferred_element_type=jnp.float32)  14.4 us
    reduce_scatter x1, waiting for transfers between devices, body(): lax.psum_scatter(jnp.dot(gathered, out_weight, preferred_element_type=jnp...  13.8 us
    ppermute x12, waiting for transfers between devices, shifted(): lax.ppermute(x, axis, [(i, (i + by) % devices) for i in range(devices)])  12 us
    dot_general x4, matrix products, stop_partial(): jnp.einsum('rkgd,jkd->rkgj', queries, key_slot, preferred_element_type=jn...  6.03 us
    dot_general x4, matrix products, stop_partial(): jnp.einsum('rkgj,jkd->rkgd', weights.astype(jnp.bfloat16), value_slot, pr...  4.97 us
    reduce_sum x4, other arithmetic, stop_partial(): block_sum = jnp.sum(weights, axis=-1)  4.42 us
  transfers between devices with their start and end apart: 16, of which 9 were waited for; matrix products, arithmetic and copies ran while one was open for 11% of the time, Pallas kernels for 0%

profile of v1, /device:TPU:0, one launch (start us, length us, event | category | flops | bytes accessed | tf_op | source)
XLA Modules:
  0.0 123.2 jit_solution(1538564413968153774)
XLA Ops:
  6.5 3.1 %collective-permute-start = (bf16[8,8192]{1,0:T(8,128)(2,1)}, bf16[8,8192]{1,0:T(8,128)(2,1)S(1)}, u32[]{:S(2)}, u32[]{:S(2)}) collective-permute-start(bf16[8,8192]{1,0:T(8,128)(2,1)} %param.5), channel_id=1, source_target_pairs={{0,4},{4,8},{8,12},{12,0},{1,5},{5,9},{9,13},{13,1},{2,6},{6,10},{... | collective-permute-start | bytes 393224 | tf_op jit(solution)/shard_map/ppermute | solution.py:11
  10.6 2.7 %fusion.9 = (f32[8,4,16]{2,0,1:T(8,128)S(1)}, f32[4,2048,8,16]{1,3,2,0:T(8,128)S(1)}) fusion(pred[8,2048]{1,0:T(8,128)(4,1)S(1)} %get-tuple-element.7, bf16[8,4,16,128]{3,0,2,1:T(8,128)(2,1)} %bitcast.149, bf16[2048,4,128,1]{2,1,0,3:T(4,128)(2,1)} %bitcast.145), kind=kOutput, calls=%fused_computation.17 | convolution fusion | flops 271580672 | bytes 6440960 | tf_op jit(solution)/shard_map/rkgd,jkd->rkgj/dot_general | solution.py:20
  13.3 1.2 %fusion.91 = bf16[1,8,4,16,128]{4,3,1,2,0:T(8,128)(2,1)S(1)} fusion(bf16[2048,4,128,1]{2,1,0,3:T(4,128)(2,1)S(1)} %bitcast.121, f32[4,2048,8,16]{1,3,2,0:T(8,128)S(1)} %get-tuple-element.22, f32[8,4,16]{2,0,1:T(8,128)S(1)} %get-tuple-element.21, pred[8,2048]{1,0:T(8,128)(4,1)S(1)} %get-tuple-element.7), kind=kOutput, calls=%fused_computation.67 | convolution fusion | flops 272695296 | bytes 6440960 | tf_op jit(solution)/shard_map/rkgj,jkd->rkgd/dot_general | solution.py:27
  17.3 1.2 %fusion.86 = bf16[8,4,16,128]{3,2,0,1:T(8,128)(2,1)S(1)} fusion(bf16[2048,4,128,1]{2,1,0,3:T(4,128)(2,1)S(1)} %bitcast.124, f32[4,2048,8,16]{1,3,2,0:T(8,128)S(1)} %get-tuple-element.20, f32[8,4,16]{2,0,1:T(8,128)S(1)} %get-tuple-element.19, pred[8,2048]{1,0:T(8,128)(4,1)S(1)} %get-tuple-element.8), kind=kOutput, calls=%fused_computation.66 | convolution fusion | flops 272695296 | bytes 6440960 | tf_op jit(solution)/shard_map/rkgj,jkd->rkgd/dot_general | solution.py:27
  18.5 1.6 %collective-permute-start.2 = (bf16[8,8192]{1,0:T(8,128)(2,1)S(1)}, bf16[8,8192]{1,0:T(8,128)(2,1)S(1)}, u32[]{:S(2)}, u32[]{:S(2)}) collective-permute-start(bf16[8,8192]{1,0:T(8,128)(2,1)S(1)} %collective-permute-done), channel_id=1, source_target_pairs={{0,4},{4,8},{8,12},{12,0},{1,5},{5,9},{9,13},{13,1},{2,6},{6,10},{... | collective-permute-start | bytes 393224 | tf_op jit(solution)/shard_map/ppermute | solution.py:11
  21.2 2.3 %collective-permute-start.1 = (f32[8,4,16]{2,0,1:T(8,128)S(1)}, f32[8,4,16]{2,0,1:T(8,128)S(1)}, u32[]{:S(2)}, u32[]{:S(2)}) collective-permute-start(f32[8,4,16]{2,0,1:T(8,128)S(1)} %get-tuple-element.19), channel_id=1, source_target_pairs={{0,12},{4,0},{8,4},{12,8},{1,13},{5,1},{9,5},{13,9},{2,14},{6,2},{... | collective-permute-start | bytes 6152 | tf_op jit(solution)/shard_map/ppermute | solution.py:11
  23.8 2.0 %collective-permute-start.6 = (bf16[8,4,16,128]{3,2,0,1:T(8,128)(2,1)S(1)}, bf16[8,4,16,128]{3,2,0,1:T(8,128)(2,1)S(1)}, u32[]{:S(2)}, u32[]{:S(2)}) collective-permute-start(bf16[8,4,16,128]{3,2,0,1:T(8,128)(2,1)S(1)} %fusion.86), channel_id=1, source_target_pairs={{0,12},{4,0},{8,4},{12,8},{1,13},{5,1},{9,5},{13,9},{2,14},{6,2},{... | collective-permute-start | bytes 393224 | tf_op jit(solution)/shard_map/ppermute | solution.py:11
  25.8 1.1 fusion.3
  26.9 1.2 %fusion.81 = bf16[8,4,16,128]{3,2,0,1:T(8,128)(2,1)S(1)} fusion(bf16[2048,4,128,1]{2,1,0,3:T(4,128)(2,1)S(1)} %bitcast.123, f32[4,2048,8,16]{1,3,2,0:T(8,128)S(1)} %get-tuple-element.18, f32[8,4,16]{2,0,1:T(8,128)S(1)} %get-tuple-element.17, pred[8,2048]{1,0:T(8,128)(4,1)S(1)} %get-tuple-element.9), kind=kOutput, calls=%fused_computation.65 | convolution fusion | flops 272695296 | bytes 6440960 | tf_op jit(solution)/shard_map/rkgj,jkd->rkgd/dot_general | solution.py:27
  29.5 1.2 collective-permute-start.3
  30.8 4.5 %collective-permute-done.4 = bf16[8,8192]{1,0:T(8,128)(2,1)S(1)} collective-permute-done((bf16[8,8192]{1,0:T(8,128)(2,1)S(1)}, bf16[8,8192]{1,0:T(8,128)(2,1)S(1)}, u32[]{:S(2)}, u32[]{:S(2)}) %collective-permute-start.4) | collective-permute-done | bytes 131104 | tf_op jit(solution)/shard_map/ppermute | solution.py:11
  35.3 1.1 fusion
  36.5 1.2 %fusion.76 = bf16[8,4,16,128]{3,2,0,1:T(8,128)(2,1)S(1)} fusion(bf16[2048,4,128,1]{2,1,0,3:T(4,128)(2,1)S(1)} %bitcast.122, f32[4,2048,8,16]{1,3,2,0:T(8,128)S(1)} %get-tuple-element.16, f32[8,4,16]{2,0,1:T(8,128)S(1)} %get-tuple-element.15, pred[8,2048]{1,0:T(8,128)(4,1)S(1)} %get-tuple-element.10), kind=kOutput, calls=%fused_computation.64 | convolution fusion | flops 272695296 | bytes 6440960 | tf_op jit(solution)/shard_map/rkgj,jkd->rkgd/dot_general | solution.py:27
  39.0 2.8 %collective-permute-start.7 = (bf16[8,4,16,128]{3,2,0,1:T(8,128)(2,1)S(1)}, bf16[8,4,16,128]{3,2,0,1:T(8,128)(2,1)S(1)}, u32[]{:S(2)}, u32[]{:S(2)}) collective-permute-start(bf16[8,4,16,128]{3,2,0,1:T(8,128)(2,1)S(1)} %fusion.81), channel_id=1, source_target_pairs={{0,8},{4,12},{8,0},{12,4},{1,9},{5,13},{9,1},{13,5},{2,10},{6,14},... | collective-permute-start | bytes 393224 | tf_op jit(solution)/shard_map/ppermute | solution.py:11
  42.1 1.2 collective-permute-start.11
  43.4 2.8 %collective-permute-done.10 = f32[8,4,16]{2,0,1:T(8,128)S(1)} collective-permute-done((f32[8,4,16]{2,0,1:T(8,128)S(1)}, f32[8,4,16]{2,0,1:T(8,128)S(1)}, u32[]{:S(2)}, u32[]{:S(2)}) %collective-permute-start.10) | collective-permute-done | bytes 2080 | tf_op jit(solution)/shard_map/ppermute | solution.py:11
  46.2 2.6 %collective-permute-done.11 = f32[8,4,16]{2,0,1:T(8,128)S(1)} collective-permute-done((f32[8,4,16]{2,0,1:T(8,128)S(1)}, f32[8,4,16]{2,0,1:T(8,128)S(1)}, u32[]{:S(2)}, u32[]{:S(2)}) %collective-permute-start.11) | collective-permute-done | bytes 2080 | tf_op jit(solution)/shard_map/ppermute | solution.py:11
  48.9 1.7 %collective-permute-done.7 = bf16[8,4,16,128]{3,2,0,1:T(8,128)(2,1)S(1)} collective-permute-done((bf16[8,4,16,128]{3,2,0,1:T(8,128)(2,1)S(1)}, bf16[8,4,16,128]{3,2,0,1:T(8,128)(2,1)S(1)}, u32[]{:S(2)}, u32[]{:S(2)}) %collective-permute-start.7) | collective-permute-done | bytes 131104 | tf_op jit(solution)/shard_map/ppermute | solution.py:11
  51.3 1.3 %collective-permute-done.12 = bf16[8,8192]{1,0:T(8,128)(2,1)S(1)} collective-permute-done((bf16[8,8192]{1,0:T(8,128)(2,1)S(1)}, bf16[8,8192]{1,0:T(8,128)(2,1)S(1)}, u32[]{:S(2)}, u32[]{:S(2)}) %collective-permute-start.12) | collective-permute-done | bytes 131104 | tf_op jit(solution)/shard_map/ppermute | solution.py:81
  52.8 8.3 %collective-permute-done.13 = bf16[16,8192]{1,0:T(8,128)(2,1)S(1)} collective-permute-done((bf16[16,8192]{1,0:T(8,128)(2,1)S(1)}, bf16[16,8192]{1,0:T(8,128)(2,1)S(1)}, u32[]{:S(2)}, u32[]{:S(2)}) %collective-permute-start.13) | collective-permute-done | bytes 262176 | tf_op jit(solution)/shard_map/ppermute | solution.py:81
  62.3 24.3 %collective-permute-done.14 = bf16[32,8192]{1,0:T(8,128)(2,1)S(1)} collective-permute-done((bf16[32,8192]{1,0:T(8,128)(2,1)S(1)}, bf16[32,8192]{1,0:T(8,128)(2,1)S(1)}, u32[]{:S(2)}, u32[]{:S(2)}) %collective-permute-start.14) | collective-permute-done | bytes 524320 | tf_op jit(solution)/shard_map/ppermute | solution.py:81
  86.5 14.4 %fusion.96 = f32[64,2048]{1,0:T(8,128)} fusion(bf16[8192,2048]{1,0:T(8,128)(2,1)} %param.9, bf16[32,8192]{1,0:T(8,128)(2,1)S(1)} %collective-permute-done.14, bf16[32,8192]{1,0:T(8,128)(2,1)S(1)} %maximum_select_fusion.2, pred[]{:T(512)S(6)} %eq.14), kind=kOutput, calls=%fused_computation.69 | convolution fusion | flops 2152202240 | bytes 35127296 | tf_op jit(solution)/shard_map/dot_general | solution.py:89
  100.9 13.8 %reduce-scatter.2.cloned.1.call-done = f32[32,2048]{1,0:T(8,128)} async-done(((f32[64,2048]{1,0:T(8,128)}), f32[32,2048]{1,0:T(8,128)}) %reduce-scatter.2.cloned.1.call-update) | async-done | bytes 262160 | tf_op jit(solution)/shard_map/reduce_scatter | solution.py:88
  114.7 1.6 %convert_element_type.64 = bf16[32,2048]{1,0:T(8,128)(2,1)} convert(f32[32,2048]{1,0:T(8,128)} %reduce-scatter.2.cloned.1.call-done) | non-fusion elementwise | flops 65536 | bytes 393216 | tf_op jit(solution)/shard_map/convert_element_type | solution.py:94
  (41 shorter events, 10.2 us)
Async XLA Ops:
  6.5 6.8 %copy-start = (bf16[1,1,2048,4,128]{4,3,2,1,0:T(4,128)(2,1)S(1)}, bf16[1,1,2048,4,128]{4,3,2,1,0:T(4,128)(2,1)}, u32[]{:S(2)}) copy-start(bf16[1,1,2048,4,128]{4,3,2,1,0:T(4,128)(2,1)} %param.7) | copy-start | bytes 6291460
  6.5 108.2 %reduce-scatter.2.cloned.1.call-start = ((), (), s32[]{:S(2)}) async-start(), calls=%async_computation.1 | async-start | bytes 786432 | tf_op jit(solution)/shard_map/reduce_scatter | solution.py:88
  6.5 9.1 %collective-permute-start = (bf16[8,8192]{1,0:T(8,128)(2,1)}, bf16[8,8192]{1,0:T(8,128)(2,1)S(1)}, u32[]{:S(2)}, u32[]{:S(2)}) collective-permute-start(bf16[8,8192]{1,0:T(8,128)(2,1)} %param.5), channel_id=1, source_target_pairs={{0,4},{4,8},{8,12},{12,0},{1,5},{5,9},{9,13},{13,1},{2,6},{6,10},{... | collective-permute-start | bytes 393224 | tf_op jit(solution)/shard_map/ppermute | solution.py:11
  14.5 1.6 %copy-start.1 = (bf16[1,1,2048,4,128]{4,3,2,1,0:T(4,128)(2,1)S(1)}, bf16[1,1,2048,4,128]{4,3,2,1,0:T(4,128)(2,1)}, u32[]{:S(2)}) copy-start(bf16[1,1,2048,4,128]{4,3,2,1,0:T(4,128)(2,1)} %param.6) | copy-start | bytes 6291460
  18.5 7.3 %collective-permute-start.2 = (bf16[8,8192]{1,0:T(8,128)(2,1)S(1)}, bf16[8,8192]{1,0:T(8,128)(2,1)S(1)}, u32[]{:S(2)}, u32[]{:S(2)}) collective-permute-start(bf16[8,8192]{1,0:T(8,128)(2,1)S(1)} %collective-permute-done), channel_id=1, source_target_pairs={{0,4},{4,8},{8,12},{12,0},{1,5},{5,9},{9,13},{13,1},{2,6},{6,10},{... | collective-permute-start | bytes 393224 | tf_op jit(solution)/shard_map/ppermute | solution.py:11
  21.2 17.6 %collective-permute-start.1 = (f32[8,4,16]{2,0,1:T(8,128)S(1)}, f32[8,4,16]{2,0,1:T(8,128)S(1)}, u32[]{:S(2)}, u32[]{:S(2)}) collective-permute-start(f32[8,4,16]{2,0,1:T(8,128)S(1)} %get-tuple-element.19), channel_id=1, source_target_pairs={{0,12},{4,0},{8,4},{12,8},{1,13},{5,1},{9,5},{13,9},{2,14},{6,2},{... | collective-permute-start | bytes 6152 | tf_op jit(solution)/shard_map/ppermute | solution.py:11
  23.5 19.8 %collective-permute-start.9 = (f32[8,4,16]{2,0,1:T(8,128)S(1)}, f32[8,4,16]{2,0,1:T(8,128)S(1)}, u32[]{:S(2)}, u32[]{:S(2)}) collective-permute-start(f32[8,4,16]{2,0,1:T(8,128)S(1)} %fusion.14), channel_id=1, source_target_pairs={{0,12},{4,0},{8,4},{12,8},{1,13},{5,1},{9,5},{13,9},{2,14},{6,2},{... | collective-permute-start | bytes 6152 | tf_op jit(solution)/shard_map/ppermute | solution.py:11
  23.8 25.0 %collective-permute-start.6 = (bf16[8,4,16,128]{3,2,0,1:T(8,128)(2,1)S(1)}, bf16[8,4,16,128]{3,2,0,1:T(8,128)(2,1)S(1)}, u32[]{:S(2)}, u32[]{:S(2)}) collective-permute-start(bf16[8,4,16,128]{3,2,0,1:T(8,128)(2,1)S(1)} %fusion.86), channel_id=1, source_target_pairs={{0,12},{4,0},{8,4},{12,8},{1,13},{5,1},{9,5},{13,9},{2,14},{6,2},{... | collective-permute-start | bytes 393224 | tf_op jit(solution)/shard_map/ppermute | solution.py:11
  28.2 7.1 %collective-permute-start.4 = (bf16[8,8192]{1,0:T(8,128)(2,1)S(1)}, bf16[8,8192]{1,0:T(8,128)(2,1)S(1)}, u32[]{:S(2)}, u32[]{:S(2)}) collective-permute-start(bf16[8,8192]{1,0:T(8,128)(2,1)S(1)} %collective-permute-done.2), channel_id=1, source_target_pairs={{0,4},{4,8},{8,12},{12,0},{1,5},{5,9},{9,13},{13,1},{2,6},{6,10},{... | collective-permute-start | bytes 393224 | tf_op jit(solution)/shard_map/ppermute | solution.py:11
  29.5 9.4 %collective-permute-start.3 = (f32[8,4,16]{2,0,1:T(8,128)S(1)}, f32[8,4,16]{2,0,1:T(8,128)S(1)}, u32[]{:S(2)}, u32[]{:S(2)}) collective-permute-start(f32[8,4,16]{2,0,1:T(8,128)S(1)} %get-tuple-element.17), channel_id=1, source_target_pairs={{0,8},{4,12},{8,0},{12,4},{1,9},{5,13},{9,1},{13,5},{2,10},{6,14},... | collective-permute-start | bytes 6152 | tf_op jit(solution)/shard_map/ppermute | solution.py:11
  36.4 5.7 %collective-permute-start.5 = (f32[8,4,16]{2,0,1:T(8,128)S(1)}, f32[8,4,16]{2,0,1:T(8,128)S(1)}, u32[]{:S(2)}, u32[]{:S(2)}) collective-permute-start(f32[8,4,16]{2,0,1:T(8,128)S(1)} %get-tuple-element.15), channel_id=1, source_target_pairs={{0,4},{4,8},{8,12},{12,0},{1,5},{5,9},{9,13},{13,1},{2,6},{6,10},{... | collective-permute-start | bytes 6152 | tf_op jit(solution)/shard_map/ppermute | solution.py:11
  38.8 7.4 %collective-permute-start.10 = (f32[8,4,16]{2,0,1:T(8,128)S(1)}, f32[8,4,16]{2,0,1:T(8,128)S(1)}, u32[]{:S(2)}, u32[]{:S(2)}) collective-permute-start(f32[8,4,16]{2,0,1:T(8,128)S(1)} %fusion.16), channel_id=1, source_target_pairs={{0,8},{4,12},{8,0},{12,4},{1,9},{5,13},{9,1},{13,5},{2,10},{6,14},... | collective-permute-start | bytes 6152 | tf_op jit(solution)/shard_map/ppermute | solution.py:11
  39.0 11.6 %collective-permute-start.7 = (bf16[8,4,16,128]{3,2,0,1:T(8,128)(2,1)S(1)}, bf16[8,4,16,128]{3,2,0,1:T(8,128)(2,1)S(1)}, u32[]{:S(2)}, u32[]{:S(2)}) collective-permute-start(bf16[8,4,16,128]{3,2,0,1:T(8,128)(2,1)S(1)} %fusion.81), channel_id=1, source_target_pairs={{0,8},{4,12},{8,0},{12,4},{1,9},{5,13},{9,1},{13,5},{2,10},{6,14},... | collective-permute-start | bytes 393224 | tf_op jit(solution)/shard_map/ppermute | solution.py:11
  42.1 6.7 %collective-permute-start.11 = (f32[8,4,16]{2,0,1:T(8,128)S(1)}, f32[8,4,16]{2,0,1:T(8,128)S(1)}, u32[]{:S(2)}, u32[]{:S(2)}) collective-permute-start(f32[8,4,16]{2,0,1:T(8,128)S(1)} %fusion.18), channel_id=1, source_target_pairs={{0,4},{4,8},{8,12},{12,0},{1,5},{5,9},{9,13},{13,1},{2,6},{6,10},{... | collective-permute-start | bytes 6152 | tf_op jit(solution)/shard_map/ppermute | solution.py:11
  43.3 7.3 %collective-permute-start.8 = (bf16[8,4,16,128]{3,2,0,1:T(8,128)(2,1)S(1)}, bf16[8,4,16,128]{3,2,0,1:T(8,128)(2,1)S(1)}, u32[]{:S(2)}, u32[]{:S(2)}) collective-permute-start(bf16[8,4,16,128]{3,2,0,1:T(8,128)(2,1)S(1)} %fusion.76), channel_id=1, source_target_pairs={{0,4},{4,8},{8,12},{12,0},{1,5},{5,9},{9,13},{13,1},{2,6},{6,10},{... | collective-permute-start | bytes 393224 | tf_op jit(solution)/shard_map/ppermute | solution.py:11
  51.2 1.4 %collective-permute-start.12 = (bf16[8,8192]{1,0:T(8,128)(2,1)S(1)}, bf16[8,8192]{1,0:T(8,128)(2,1)S(1)}, u32[]{:S(2)}, u32[]{:S(2)}) collective-permute-start(bf16[8,8192]{1,0:T(8,128)(2,1)S(1)} %bitcast.125), channel_id=1, source_target_pairs={{0,1},{1,0},{4,5},{5,4},{8,9},{9,8},{12,13},{13,12},{2,3},{3,2},{6... | collective-permute-start | bytes 393224 | tf_op jit(solution)/shard_map/ppermute | solution.py:81
  52.7 8.4 %collective-permute-start.13 = (bf16[16,8192]{1,0:T(8,128)(2,1)S(1)}, bf16[16,8192]{1,0:T(8,128)(2,1)S(1)}, u32[]{:S(2)}, u32[]{:S(2)}) collective-permute-start(bf16[16,8192]{1,0:T(8,128)(2,1)S(1)} %maximum_select_fusion.3), channel_id=1, source_target_pairs={{0,4},{1,5},{4,0},{5,1},{8,12},{9,13},{12,8},{13,9},{2,6},{3,7},{6... | collective-permute-start | bytes 786440 | tf_op jit(solution)/shard_map/ppermute | solution.py:81
  61.2 25.3 %collective-permute-start.14 = (bf16[32,8192]{1,0:T(8,128)(2,1)S(1)}, bf16[32,8192]{1,0:T(8,128)(2,1)S(1)}, u32[]{:S(2)}, u32[]{:S(2)}) collective-permute-start(bf16[32,8192]{1,0:T(8,128)(2,1)S(1)} %maximum_select_fusion.2), channel_id=1, source_target_pairs={{0,8},{1,9},{4,12},{5,13},{8,0},{9,1},{12,4},{13,5},{2,10},{3,11},... | collective-permute-start | bytes 1572872 | tf_op jit(solution)/shard_map/ppermute | solution.py:81
Sparse Core Ops, SparseCore 0:
  101.0 13.6 reduce-scatter.1
